TPU v7x, 32 devices: a whole 2x2x4 slice. The times are simulated.
32 devices in a mesh: tp: 8 (over z, y), dp: 4 (over x, core).
Axes of the slice: x: 2, y: 2, z: 4, core: 2. Of those that a mesh axis runs over, the one named last changes fastest.
Arguments:
- tokens: bfloat16 [4, 16, 4096], P('dp', 'tp'), may hold values from -6 to 6
- gate_weight: bfloat16 [4096, 16384], P('dp', 'tp'), may hold values from -0.09375 to 0.09375
- up_weight: bfloat16 [4096, 16384], P('dp', 'tp'), may hold values from -0.09375 to 0.09375
- cotangent: bfloat16 [4, 16, 16384], P('dp', None, 'tp'), may hold values from -6 to 6
Outputs:
- hidden: bfloat16 [4, 16, 16384], P('dp', None, 'tp')
- grad_tokens: bfloat16 [4, 16, 4096], P('dp', 'tp')
- grad_gate: bfloat16 [4096, 16384], P(None, 'tp')
- grad_up: bfloat16 [4096, 16384], P(None, 'tp')
All inputs are finite; a program needn't handle non-finite values.
Results may differ from a plain program's by a relative error of at most 0.009.
Values may be sent and summed in bfloat16 or wider, within the bound.
No kernel may reach another device: no remote copies, remote signals or barrier semaphores. Data moves between devices by JAX's collectives and lax.ppermute only.
A program may use at most 320 MiB of HBM per device.

v0:
```python
import jax
import jax.numpy as jnp
from jax import lax
from jax.sharding import PartitionSpec as P


def swish_parts(gate_pre):
    sigmoid_val = jax.nn.sigmoid(gate_pre)
    return (gate_pre * sigmoid_val, sigmoid_val * (1.0 + gate_pre * (1.0 - sigmoid_val)))


def shards(tokens, gate_weight, up_weight, cotangent):
    gate_full, up_full = (
        lax.all_gather(gate_weight, "dp", axis=0, tiled=True),
        lax.all_gather(up_weight, "dp", axis=0, tiled=True),
    )
    gathered = lax.all_gather(tokens, "tp", axis=1, tiled=True)
    flat_rows = gathered[0]
    gate_pre = jnp.dot(flat_rows, gate_full, preferred_element_type=jnp.float32)
    up_pre = jnp.dot(flat_rows, up_full, preferred_element_type=jnp.float32)
    swish_act, swish_slope = swish_parts(gate_pre)
    hidden = (swish_act * up_pre).astype(jnp.bfloat16)
    back_float = cotangent[0].astype(jnp.float32)
    d_gate = (back_float * up_pre * swish_slope).astype(jnp.bfloat16)
    d_up = (back_float * swish_act).astype(jnp.bfloat16)
    across = (((1,), (1,)), ((), ()))
    down_rows = (((0,), (0,)), ((), ()))
    result = lax.dot_general(d_gate, gate_full, across, preferred_element_type=jnp.float32)
    grad_rows = lax.psum_scatter(
        result + lax.dot_general(d_up, up_full, across, preferred_element_type=jnp.float32),
        "tp",
        scatter_dimension=0,
        tiled=True,
    )
    grad_tokens = grad_rows.astype(jnp.bfloat16)[None]
    inverse_dp = 1.0 / lax.axis_size("dp")
    rows_p = lax.all_gather(gathered, "dp", axis=0, tiled=True)
    gate_p = lax.all_gather(d_gate[None], "dp", axis=0, tiled=True)
    up_p = lax.all_gather(d_up[None], "dp", axis=0, tiled=True)
    acc_gate = jnp.zeros(gate_full.shape, jnp.float32)
    acc_up = jnp.zeros(up_full.shape, jnp.float32)
    for replica in range(rows_p.shape[0]):
        term_gate = lax.dot_general(
            rows_p[replica], gate_p[replica], down_rows, preferred_element_type=jnp.float32
        )
        term_up = lax.dot_general(
            rows_p[replica], up_p[replica], down_rows, preferred_element_type=jnp.float32
        )
        acc_gate = acc_gate + lax.optimization_barrier(term_gate.astype(jnp.bfloat16)).astype(
            jnp.float32
        )
        acc_up = acc_up + lax.optimization_barrier(term_up.astype(jnp.bfloat16)).astype(jnp.float32)
    grad_gate = (acc_gate * inverse_dp).astype(jnp.bfloat16)
    grad_up = (acc_up * inverse_dp).astype(jnp.bfloat16)
    return (hidden[None], grad_tokens, grad_gate, grad_up)


def solution(mesh):
    in_specs = (P("dp", "tp", None), P("dp", "tp"), P("dp", "tp"), P("dp", None, "tp"))
    out_specs = (P("dp", None, "tp"), P("dp", "tp", None), P(None, "tp"), P(None, "tp"))
    return jax.shard_map(shards, mesh=mesh, in_specs=in_specs, out_specs=out_specs, check_vma=False)
```

profile of v0, /device:TPU:0, one launch (start us, length us, event | category | flops | bytes accessed | tf_op | source)
XLA Modules:
  0.0 485.2 jit_solution(3672661935274794439)
XLA Ops:
  7.2 0.0 copy-start
  7.2 0.0 all-gather.7.cloned.1.call-start
  7.2 0.7 all-gather.7.cloned.1.call-update
  7.9 0.0 all-gather.5.cloned.1.call-start
  8.0 0.7 all-gather.5.cloned.1.call-update
  8.7 0.7 copy.14
  9.4 32.6 %all_gather.18 = bf16[1,16,4096]{2,0,1:T(2,128)(2,1)S(1)} all-gather(bf16[1,2,4096]{2,0,1:T(2,128)(2,1)S(1)} %copy.14), channel_id=1, replica_groups=mesh['tp'=8,'dp'=4] {'tp'}, dimensions={1}, use_global_device_ids=true | all-gather | bytes 147456 | tf_op jit(solution)/shard_map/all_gather | solution.py:17
  42.0 0.1 copy.18
  42.1 1.2 dynamic-slice
  44.0 10.5 %all_gather.22 = bf16[4,16,4096]{2,1,0:T(8,128)(2,1)S(1)} all-gather(bf16[1,16,4096]{2,1,0:T(8,128)(2,1)S(1)} %copy.18), channel_id=1, replica_groups=mesh['tp'=8,'dp'=4] {'dp'}, dimensions={0}, use_global_device_ids=true | all-gather | bytes 655360 | tf_op jit(solution)/shard_map/all_gather | solution.py:37
  54.5 66.5 %all-gather.7.cloned.1.call-done = bf16[4096,2048]{1,0:T(8,128)(2,1)} async-done(((bf16[1024,2048]{1,0:T(8,128)(2,1)}), bf16[4096,2048]{1,0:T(8,128)(2,1)}) %all-gather.7.cloned.1.call-update) | async-done | bytes 16777232 | tf_op jit(solution)/shard_map/all_gather | solution.py:15
  121.0 8.0 %fusion.3 = f32[16,2048]{1,0:T(8,128)S(1)} fusion(bf16[4096,2048]{1,0:T(8,128)(2,1)} %all-gather.7.cloned.1.call-done, bf16[1,16,4096]{2,1,0:T(8,128)(2,1)S(1)} %copy.18), kind=kOutput, calls=%fused_computation.20 | convolution fusion | flops 268435456 | bytes 17039360 | tf_op jit(solution)/shard_map/dot_general | solution.py:20
  129.0 99.4 %all-gather.5.cloned.1.call-done = bf16[4096,2048]{1,0:T(8,128)(2,1)} async-done(((bf16[1024,2048]{1,0:T(8,128)(2,1)}), bf16[4096,2048]{1,0:T(8,128)(2,1)}) %all-gather.5.cloned.1.call-update) | async-done | bytes 16777232 | tf_op jit(solution)/shard_map/all_gather | solution.py:14
  228.5 8.7 %fusion.1 = (bf16[16,2048]{1,0:T(8,128)(2,1)S(1)}, bf16[1,16,2048]{2,1,0:T(8,128)(2,1)}, bf16[16,2048]{1,0:T(8,128)(2,1)S(1)}) fusion(f32[16,2048]{1,0:T(8,128)S(1)} %fusion.3, bf16[1,16,2048]{2,1,0:T(8,128)(2,1)S(1)} %copy-done, bf16[4096,2048]{1,0:T(8,128)(2,1)} %all-gather.5.cloned.1.call-done, bf16[1,16,4096]{2,1,0:T(8,128)(2,1)S(1)} %copy.18), kind=kOutput, calls=%fused_computation.14 | convolution fusion | flops 268959744 | bytes 17301504 | tf_op jit(solution)/shard_map/dot_general | solution.py:19
  237.2 5.9 %all-gather.1 = bf16[64,2048]{1,0:T(8,128)(2,1)S(1)} all-gather(bf16[16,2048]{1,0:T(8,128)(2,1)S(1)} %get-tuple-element.18), channel_id=3, replica_groups=mesh['tp'=8,'dp'=4] {'dp'}, dimensions={0}, use_global_device_ids=true | all-gather | bytes 327680 | tf_op jit(solution)/shard_map/all_gather | solution.py:39
  243.1 8.5 %convert_bitcast_fusion = bf16[4096,2048]{0,1:T(8,128)(2,1)} fusion(bf16[4,16,4096]{2,1,0:T(8,128)(2,1)S(1)} %all_gather.22, bf16[64,2048]{1,0:T(8,128)(2,1)S(1)} %all-gather.1), kind=kOutput, calls=%fused_computation.2 | convolution fusion | flops 276824064 | bytes 16973824 | tf_op jit(solution)/shard_map/dot_general | solution.py:46
  251.7 8.1 %convert_bitcast_fusion.1 = bf16[4096,2048]{0,1:T(8,128)(2,1)} fusion(bf16[4,16,4096]{2,1,0:T(8,128)(2,1)S(1)} %all_gather.22, bf16[64,2048]{1,0:T(8,128)(2,1)S(1)} %all-gather.1), kind=kOutput, calls=%fused_computation.3 | convolution fusion | flops 276824064 | bytes 16973824 | tf_op jit(solution)/shard_map/dot_general | solution.py:46
  259.7 8.0 %convert_bitcast_fusion.2 = bf16[4096,2048]{0,1:T(8,128)(2,1)} fusion(bf16[4,16,4096]{2,1,0:T(8,128)(2,1)S(1)} %all_gather.22, bf16[64,2048]{1,0:T(8,128)(2,1)S(1)} %all-gather.1), kind=kOutput, calls=%fused_computation.4 | convolution fusion | flops 276824064 | bytes 16973824 | tf_op jit(solution)/shard_map/dot_general | solution.py:46
  267.8 8.0 %convert_bitcast_fusion.3 = bf16[4096,2048]{0,1:T(8,128)(2,1)} fusion(bf16[4,16,4096]{2,1,0:T(8,128)(2,1)S(1)} %all_gather.22, bf16[64,2048]{1,0:T(8,128)(2,1)S(1)} %all-gather.1), kind=kOutput, calls=%fused_computation.5 | convolution fusion | flops 276824064 | bytes 16973824 | tf_op jit(solution)/shard_map/dot_general | solution.py:46
  275.8 6.0 %all-gather = bf16[64,2048]{1,0:T(8,128)(2,1)S(1)} all-gather(bf16[16,2048]{1,0:T(8,128)(2,1)S(1)} %get-tuple-element.16), channel_id=2, replica_groups=mesh['tp'=8,'dp'=4] {'dp'}, dimensions={0}, use_global_device_ids=true | all-gather | bytes 327680 | tf_op jit(solution)/shard_map/all_gather | solution.py:38
  281.9 8.5 %convert_bitcast_fusion.4 = bf16[4096,2048]{0,1:T(8,128)(2,1)} fusion(bf16[4,16,4096]{2,1,0:T(8,128)(2,1)S(1)} %all_gather.22, bf16[64,2048]{1,0:T(8,128)(2,1)S(1)} %all-gather), kind=kOutput, calls=%fused_computation.6 | convolution fusion | flops 276824064 | bytes 16973824 | tf_op jit(solution)/shard_map/dot_general | solution.py:43
  290.4 8.1 %convert_bitcast_fusion.5 = bf16[4096,2048]{0,1:T(8,128)(2,1)} fusion(bf16[4,16,4096]{2,1,0:T(8,128)(2,1)S(1)} %all_gather.22, bf16[64,2048]{1,0:T(8,128)(2,1)S(1)} %all-gather), kind=kOutput, calls=%fused_computation.7 | convolution fusion | flops 276824064 | bytes 16973824 | tf_op jit(solution)/shard_map/dot_general | solution.py:43
  298.5 8.1 %convert_bitcast_fusion.6 = bf16[4096,2048]{0,1:T(8,128)(2,1)} fusion(bf16[4,16,4096]{2,1,0:T(8,128)(2,1)S(1)} %all_gather.22, bf16[64,2048]{1,0:T(8,128)(2,1)S(1)} %all-gather), kind=kOutput, calls=%fused_computation.8 | convolution fusion | flops 276824064 | bytes 16973824 | tf_op jit(solution)/shard_map/dot_general | solution.py:43
  306.5 8.1 %convert_bitcast_fusion.7 = bf16[4096,2048]{0,1:T(8,128)(2,1)} fusion(bf16[4,16,4096]{2,1,0:T(8,128)(2,1)S(1)} %all_gather.22, bf16[64,2048]{1,0:T(8,128)(2,1)S(1)} %all-gather), kind=kOutput, calls=%fused_computation.9 | convolution fusion | flops 276824064 | bytes 16973824 | tf_op jit(solution)/shard_map/dot_general | solution.py:43
  314.6 10.2 %fusion.20 = f32[16,4096]{1,0:T(8,128)S(1)} fusion(bf16[16,2048]{1,0:T(8,128)(2,1)S(1)} %get-tuple-element.16, bf16[4096,2048]{1,0:T(8,128)(2,1)} %all-gather.5.cloned.1.call-done), kind=kOutput, calls=%fused_computation.38 | convolution fusion | flops 268435456 | bytes 17104896 | tf_op jit(solution)/shard_map/dot_general | solution.py:28
  324.8 10.2 %convolution_add_fusion = f32[16,4096]{1,0:T(8,128)S(1)} fusion(f32[16,4096]{1,0:T(8,128)S(1)} %fusion.20, bf16[16,2048]{1,0:T(8,128)(2,1)S(1)} %get-tuple-element.18, bf16[4096,2048]{1,0:T(8,128)(2,1)} %all-gather.7.cloned.1.call-done), kind=kOutput, calls=%fused_computation.10 | convolution fusion | flops 268500992 | bytes 17367040 | tf_op jit(solution)/shard_map/dot_general | solution.py:30
  335.0 40.4 %all-reduce.2 = bf16[16,4096]{1,0:T(8,128)(2,1)S(1)} all-reduce(f32[16,4096]{1,0:T(8,128)S(1)} %convolution_add_fusion), channel_id=4, replica_groups=mesh['tp'=8,'dp'=4] {'tp'}, use_global_device_ids=true, to_apply=%region_0.0.clone | all-reduce | flops 65536 | bytes 393216
  375.4 28.7 %multiply_convert_fusion = bf16[4096,2048]{0,1:T(8,128)(2,1)} fusion(bf16[4096,2048]{0,1:T(8,128)(2,1)} %convert_bitcast_fusion, bf16[4096,2048]{0,1:T(8,128)(2,1)} %convert_bitcast_fusion.1, bf16[4096,2048]{0,1:T(8,128)(2,1)} %convert_bitcast_fusion.2, bf16[4096,2048]{0,1:T(8,128)(2,1)} %convert_bitcast_fusion.3), kind=kLoop, calls=%fused_computation | loop fusion | flops 75497472 | bytes 83886080 | tf_op jit(solution)/shard_map/convert_element_type | solution.py:54
  404.2 22.4 %copy.17 = bf16[4096,2048]{1,0:T(8,128)(2,1)} copy(bf16[4096,2048]{0,1:T(8,128)(2,1)} %multiply_convert_fusion) | data formatting | bytes 33554432
  426.6 28.8 %multiply_convert_fusion.1 = bf16[4096,2048]{0,1:T(8,128)(2,1)} fusion(bf16[4096,2048]{0,1:T(8,128)(2,1)} %convert_bitcast_fusion.4, bf16[4096,2048]{0,1:T(8,128)(2,1)} %convert_bitcast_fusion.5, bf16[4096,2048]{0,1:T(8,128)(2,1)} %convert_bitcast_fusion.6, bf16[4096,2048]{0,1:T(8,128)(2,1)} %convert_bitcast_fusion.7), kind=kLoop, calls=%fused_computation.1 | loop fusion | flops 75497472 | bytes 83886080 | tf_op jit(solution)/shard_map/convert_element_type | solution.py:53
  455.3 22.4 %copy.16 = bf16[4096,2048]{1,0:T(8,128)(2,1)} copy(bf16[4096,2048]{0,1:T(8,128)(2,1)} %multiply_convert_fusion.1) | data formatting | bytes 33554432
  477.8 0.6 fusion.17
  (1 shorter events, 0.0 us)
Async XLA Ops:
  7.2 221.3 %copy-start = (bf16[1,16,2048]{2,1,0:T(8,128)(2,1)S(1)}, bf16[1,16,2048]{2,1,0:T(8,128)(2,1)}, u32[]{:S(2)}) copy-start(bf16[1,16,2048]{2,1,0:T(8,128)(2,1)} %param.7) | copy-start | bytes 196612
  7.2 113.8 %all-gather.7.cloned.1.call-start = ((), (), s32[]{:S(2)}) async-start(), calls=%async_computation.1 | async-start | bytes 20971520 | tf_op jit(solution)/shard_map/all_gather | solution.py:15
  7.9 220.6 %all-gather.5.cloned.1.call-start = ((), (), s32[]{:S(2)}) async-start(), calls=%async_computation | async-start | bytes 20971520 | tf_op jit(solution)/shard_map/all_gather | solution.py:14
Sparse Core Ops, SparseCore 0:
  9.5 111.4 all-gather.6
  122.6 105.8 all-gather.4
where the time goes:
time: 487 us; the launch traced here: 485 us
  waiting for transfers between devices  167 us (34%)
  matrix products  103 us (21%)
  blocking collectives  95.5 us (20%)
  other arithmetic  57.5 us (12%)
  local copies, waits for them, and re-layouts  47.6 us (10%)
  between operations  14.7 us (3%)
    all_gather x1, waiting for transfers between devices, shards(): lax.all_gather(gate_weight, 'dp', axis=0, tiled=True)  99.4 us
    all_gather x1, waiting for transfers between devices, shards(): lax.all_gather(up_weight, 'dp', axis=0, tiled=True)  66.5 us
    unnamed x7, local copies, waits for them, and re-layouts  47 us
    unnamed x1, blocking collectives  40.4 us
    dot_general x4, matrix products, shards(): lax.dot_general(rows_p[replica], gate_p[replica], down_rows, preferred_el...  32.7 us
    dot_general x4, matrix products, shards(): lax.dot_general(rows_p[replica], up_p[replica], down_rows, preferred_elem...  32.7 us
    all_gather x1, blocking collectives, shards(): gathered = lax.all_gather(tokens, 'tp', axis=1, tiled=True)  32.6 us
    convert_element_type x1, other arithmetic, shards(): grad_gate = (acc_gate * inverse_dp).astype(jnp.bfloat16)  28.8 us
  transfers between devices with their start and end apart: 2, of which 2 were waited for; matrix products, arithmetic and copies ran while one was open for 2% of the time, Pallas kernels for 0%

commit v1 on v0

--- a/solution.py
+++ b/solution.py
@@ -14,7 +14,18 @@
         lax.all_gather(gate_weight, "dp", axis=0, tiled=True),
         lax.all_gather(up_weight, "dp", axis=0, tiled=True),
     )
-    gathered = lax.all_gather(tokens, "tp", axis=1, tiled=True)
+    n_parts = lax.axis_size("tp")
+    carry_out = sorted(((q, (q + 1) % n_parts) for q in range(n_parts)))
+    o_now = tokens
+    m = 1
+    heap = [o_now]
+    while m < n_parts:
+        o_now = lax.ppermute(o_now, "tp", carry_out)
+        heap.insert(0, o_now)
+        m = m + 1
+    reply = jnp.concatenate(heap, axis=1)
+    f_now = lax.axis_index("tp") + 1
+    gathered = jnp.roll(reply, f_now * tokens.shape[1], axis=1)
     flat_rows = gathered[0]
     gate_pre = jnp.dot(flat_rows, gate_full, preferred_element_type=jnp.float32)
     up_pre = jnp.dot(flat_rows, up_full, preferred_element_type=jnp.float32)

time: 487 us -> 445 us (0.914)
  local copies, waits for them, and re-layouts: 47.6 us -> 3.74 us
  blocking collectives: 95.5 us -> 63 us
  waiting for transfers between devices: 167 us -> 196 us
    all_gather x1, waiting for transfers between devices: 99.4 us -> 53.3 us  [shards(): lax.all_gather(gate_weight, 'dp', axis=0, tiled=True)]
    unnamed x7 -> x3, local copies, waits for them, and re-layouts: 47 us -> 1.24 us
    ppermute x0 -> x7, waiting for transfers between devices: none -> 41.7 us  [shards(): o_now = lax.ppermute(o_now, 'tp', carry_out)]
    all_gather x1, waiting for transfers between devices: 66.5 us -> 99.4 us  [shards(): lax.all_gather(up_weight, 'dp', axis=0, tiled=True)]
    all_gather x1 -> x0, blocking collectives: 32.6 us -> none  [shards(): gathered = lax.all_gather(tokens, 'tp', axis=1, tiled=True)]
  transfers between devices with their start and end apart: 2 -> 9, of which waited for: 2 -> 9; matrix products, arithmetic and copies ran while one was open for 2% -> 3% of each run, Pallas kernels for 0% -> 0%
where the time goes in v1:
time: 445 us; the launch traced here: 444 us
  waiting for transfers between devices  196 us (44%)
  matrix products  103 us (23%)
  blocking collectives  63 us (14%)
  other arithmetic  61 us (14%)
  between operations  14.7 us (3%)
    all_gather x1, waiting for transfers between devices, shards(): lax.all_gather(up_weight, 'dp', axis=0, tiled=True)  99.4 us
    all_gather x1, waiting for transfers between devices, shards(): lax.all_gather(gate_weight, 'dp', axis=0, tiled=True)  53.3 us
    ppermute x7, waiting for transfers between devices, shards(): o_now = lax.ppermute(o_now, 'tp', carry_out)  41.7 us
    unnamed x1, blocking collectives  40.4 us
    dot_general x4, matrix products, shards(): lax.dot_general(rows_p[replica], up_p[replica], down_rows, preferred_elem...  32.9 us
    dot_general x4, matrix products, shards(): lax.dot_general(rows_p[replica], gate_p[replica], down_rows, preferred_el...  32.9 us
    convert_element_type x1, other arithmetic, shards(): grad_gate = (acc_gate * inverse_dp).astype(jnp.bfloat16)  30.5 us
    convert_element_type x1, other arithmetic, shards(): grad_up = (acc_up * inverse_dp).astype(jnp.bfloat16)  30.5 us
  transfers between devices with their start and end apart: 9, of which 9 were waited for; matrix products, arithmetic and copies ran while one was open for 3% of the time, Pallas kernels for 0%

profile of v1, /device:TPU:0, one launch (start us, length us, event | category | flops | bytes accessed | tf_op | source)
XLA Modules:
  0.0 444.3 jit_solution(15107727376023341547)
XLA Ops:
  7.2 0.7 all-gather.5.cloned.1.call-update
  8.0 0.7 all-gather.7.cloned.1.call-update
  8.7 3.0 collective-permute-start
  11.7 5.0 %collective-permute-done = bf16[1,2,4096]{2,1,0:T(2,128)(2,1)S(1)} collective-permute-done((bf16[1,2,4096]{2,1,0:T(2,128)(2,1)}, bf16[1,2,4096]{2,1,0:T(2,128)(2,1)S(1)}, u32[]{:S(2)}, u32[]{:S(2)}) %collective-permute-start) | collective-permute-done | bytes 16416 | tf_op jit(solution)/shard_map/ppermute | solution.py:23
  16.7 6.4 %collective-permute-done.1 = bf16[1,2,4096]{2,1,0:T(2,128)(2,1)S(1)} collective-permute-done((bf16[1,2,4096]{2,1,0:T(2,128)(2,1)S(1)}, bf16[1,2,4096]{2,1,0:T(2,128)(2,1)S(1)}, u32[]{:S(2)}, u32[]{:S(2)}) %collective-permute-start.1) | collective-permute-done | bytes 16416 | tf_op jit(solution)/shard_map/ppermute | solution.py:23
  23.1 6.4 %collective-permute-done.2 = bf16[1,2,4096]{2,1,0:T(2,128)(2,1)S(1)} collective-permute-done((bf16[1,2,4096]{2,1,0:T(2,128)(2,1)S(1)}, bf16[1,2,4096]{2,1,0:T(2,128)(2,1)S(1)}, u32[]{:S(2)}, u32[]{:S(2)}) %collective-permute-start.2) | collective-permute-done | bytes 16416 | tf_op jit(solution)/shard_map/ppermute | solution.py:23
  29.6 6.4 %collective-permute-done.3 = bf16[1,2,4096]{2,1,0:T(2,128)(2,1)S(1)} collective-permute-done((bf16[1,2,4096]{2,1,0:T(2,128)(2,1)S(1)}, bf16[1,2,4096]{2,1,0:T(2,128)(2,1)S(1)}, u32[]{:S(2)}, u32[]{:S(2)}) %collective-permute-start.3) | collective-permute-done | bytes 16416 | tf_op jit(solution)/shard_map/ppermute | solution.py:23
  36.0 6.4 %collective-permute-done.4 = bf16[1,2,4096]{2,1,0:T(2,128)(2,1)S(1)} collective-permute-done((bf16[1,2,4096]{2,1,0:T(2,128)(2,1)S(1)}, bf16[1,2,4096]{2,1,0:T(2,128)(2,1)S(1)}, u32[]{:S(2)}, u32[]{:S(2)}) %collective-permute-start.4) | collective-permute-done | bytes 16416 | tf_op jit(solution)/shard_map/ppermute | solution.py:23
  42.4 6.4 %collective-permute-done.5 = bf16[1,2,4096]{2,1,0:T(2,128)(2,1)S(1)} collective-permute-done((bf16[1,2,4096]{2,1,0:T(2,128)(2,1)S(1)}, bf16[1,2,4096]{2,1,0:T(2,128)(2,1)S(1)}, u32[]{:S(2)}, u32[]{:S(2)}) %collective-permute-start.5) | collective-permute-done | bytes 16416 | tf_op jit(solution)/shard_map/ppermute | solution.py:23
  48.9 1.2 dynamic-slice
  50.8 4.5 %collective-permute-done.6 = bf16[1,2,4096]{2,1,0:T(2,128)(2,1)S(1)} collective-permute-done((bf16[1,2,4096]{2,1,0:T(2,128)(2,1)S(1)}, bf16[1,2,4096]{2,1,0:T(2,128)(2,1)S(1)}, u32[]{:S(2)}, u32[]{:S(2)}) %collective-permute-start.6) | collective-permute-done | bytes 16416 | tf_op jit(solution)/shard_map/ppermute | solution.py:23
  55.3 1.8 concatenate.6
  57.2 10.6 %all_gather.17 = bf16[4,16,4096]{2,1,0:T(8,128)(2,1)S(1)} all-gather(bf16[1,16,4096]{2,1,0:T(8,128)(2,1)S(1)} %constant_dynamic-slice_fusion), channel_id=1, replica_groups=mesh['tp'=8,'dp'=4] {'dp'}, dimensions={0}, use_global_device_ids=true | all-gather | bytes 655360 | tf_op jit(solution)/shard_map/all_gather | solution.py:48
  67.7 53.3 %all-gather.5.cloned.1.call-done = bf16[4096,2048]{1,0:T(8,128)(2,1)} async-done(((bf16[1024,2048]{1,0:T(8,128)(2,1)}), bf16[4096,2048]{1,0:T(8,128)(2,1)}) %all-gather.5.cloned.1.call-update) | async-done | bytes 16777232 | tf_op jit(solution)/shard_map/all_gather | solution.py:14
  121.0 8.0 %fusion.5 = f32[16,2048]{1,0:T(8,128)S(1)} fusion(bf16[4096,2048]{1,0:T(8,128)(2,1)} %all-gather.5.cloned.1.call-done, bf16[1,16,4096]{2,1,0:T(8,128)(2,1)S(1)} %constant_dynamic-slice_fusion), kind=kOutput, calls=%fused_computation.22 | convolution fusion | flops 268435456 | bytes 17039360 | tf_op jit(solution)/shard_map/dot_general | solution.py:30
  129.0 99.4 %all-gather.7.cloned.1.call-done = bf16[4096,2048]{1,0:T(8,128)(2,1)} async-done(((bf16[1024,2048]{1,0:T(8,128)(2,1)}), bf16[4096,2048]{1,0:T(8,128)(2,1)}) %all-gather.7.cloned.1.call-update) | async-done | bytes 16777232 | tf_op jit(solution)/shard_map/all_gather | solution.py:15
  228.5 8.7 %fusion.1 = (bf16[16,2048]{1,0:T(8,128)(2,1)S(1)}, bf16[1,16,2048]{2,1,0:T(8,128)(2,1)}, bf16[16,2048]{1,0:T(8,128)(2,1)S(1)}) fusion(f32[16,2048]{1,0:T(8,128)S(1)} %fusion.5, bf16[1,16,2048]{2,1,0:T(8,128)(2,1)S(1)} %copy-done, bf16[4096,2048]{1,0:T(8,128)(2,1)} %all-gather.7.cloned.1.call-done, bf16[1,16,4096]{2,1,0:T(8,128)(2,1)S(1)} %constant_dynamic-slice_fusion), kind=kOutput, calls=%fused_computation.14 | convolution fusion | flops 268959744 | bytes 17301504 | tf_op jit(solution)/shard_map/dot_general | solution.py:31
  237.2 5.9 %all-gather.1 = bf16[64,2048]{1,0:T(8,128)(2,1)S(1)} all-gather(bf16[16,2048]{1,0:T(8,128)(2,1)S(1)} %get-tuple-element.6), channel_id=3, replica_groups=mesh['tp'=8,'dp'=4] {'dp'}, dimensions={0}, use_global_device_ids=true | all-gather | bytes 327680 | tf_op jit(solution)/shard_map/all_gather | solution.py:50
  243.1 8.5 %convolution_convert_fusion = bf16[4096,2048]{1,0:T(8,128)(2,1)} fusion(bf16[4,16,4096]{2,1,0:T(8,128)(2,1)S(1)} %all_gather.17, bf16[64,2048]{1,0:T(8,128)(2,1)S(1)} %all-gather.1), kind=kOutput, calls=%fused_computation.2 | convolution fusion | flops 276824064 | bytes 16973824 | tf_op jit(solution)/shard_map/dot_general | solution.py:57
  251.6 8.2 %convolution_convert_fusion.1 = bf16[4096,2048]{1,0:T(8,128)(2,1)} fusion(bf16[4,16,4096]{2,1,0:T(8,128)(2,1)S(1)} %all_gather.17, bf16[64,2048]{1,0:T(8,128)(2,1)S(1)} %all-gather.1), kind=kOutput, calls=%fused_computation.3 | convolution fusion | flops 276824064 | bytes 16973824 | tf_op jit(solution)/shard_map/dot_general | solution.py:57
  259.8 8.1 %convolution_convert_fusion.2 = bf16[4096,2048]{1,0:T(8,128)(2,1)} fusion(bf16[4,16,4096]{2,1,0:T(8,128)(2,1)S(1)} %all_gather.17, bf16[64,2048]{1,0:T(8,128)(2,1)S(1)} %all-gather.1), kind=kOutput, calls=%fused_computation.4 | convolution fusion | flops 276824064 | bytes 16973824 | tf_op jit(solution)/shard_map/dot_general | solution.py:57
  267.9 8.1 %convolution_convert_fusion.3 = bf16[4096,2048]{1,0:T(8,128)(2,1)} fusion(bf16[4,16,4096]{2,1,0:T(8,128)(2,1)S(1)} %all_gather.17, bf16[64,2048]{1,0:T(8,128)(2,1)S(1)} %all-gather.1), kind=kOutput, calls=%fused_computation.5 | convolution fusion | flops 276824064 | bytes 16973824 | tf_op jit(solution)/shard_map/dot_general | solution.py:57
  276.0 6.1 %all-gather = bf16[64,2048]{1,0:T(8,128)(2,1)S(1)} all-gather(bf16[16,2048]{1,0:T(8,128)(2,1)S(1)} %get-tuple-element.4), channel_id=2, replica_groups=mesh['tp'=8,'dp'=4] {'dp'}, dimensions={0}, use_global_device_ids=true | all-gather | bytes 327680 | tf_op jit(solution)/shard_map/all_gather | solution.py:49
  282.1 8.5 %convolution_convert_fusion.4 = bf16[4096,2048]{1,0:T(8,128)(2,1)} fusion(bf16[4,16,4096]{2,1,0:T(8,128)(2,1)S(1)} %all_gather.17, bf16[64,2048]{1,0:T(8,128)(2,1)S(1)} %all-gather), kind=kOutput, calls=%fused_computation.6 | convolution fusion | flops 276824064 | bytes 16973824 | tf_op jit(solution)/shard_map/dot_general | solution.py:54
  290.6 8.1 %convolution_convert_fusion.5 = bf16[4096,2048]{1,0:T(8,128)(2,1)} fusion(bf16[4,16,4096]{2,1,0:T(8,128)(2,1)S(1)} %all_gather.17, bf16[64,2048]{1,0:T(8,128)(2,1)S(1)} %all-gather), kind=kOutput, calls=%fused_computation.7 | convolution fusion | flops 276824064 | bytes 16973824 | tf_op jit(solution)/shard_map/dot_general | solution.py:54
  298.7 8.1 %convolution_convert_fusion.6 = bf16[4096,2048]{1,0:T(8,128)(2,1)} fusion(bf16[4,16,4096]{2,1,0:T(8,128)(2,1)S(1)} %all_gather.17, bf16[64,2048]{1,0:T(8,128)(2,1)S(1)} %all-gather), kind=kOutput, calls=%fused_computation.8 | convolution fusion | flops 276824064 | bytes 16973824 | tf_op jit(solution)/shard_map/dot_general | solution.py:54
  306.8 8.2 %convolution_convert_fusion.7 = bf16[4096,2048]{1,0:T(8,128)(2,1)} fusion(bf16[4,16,4096]{2,1,0:T(8,128)(2,1)S(1)} %all_gather.17, bf16[64,2048]{1,0:T(8,128)(2,1)S(1)} %all-gather), kind=kOutput, calls=%fused_computation.9 | convolution fusion | flops 276824064 | bytes 16973824 | tf_op jit(solution)/shard_map/dot_general | solution.py:54
  315.0 10.2 %fusion.20 = f32[16,4096]{1,0:T(8,128)S(1)} fusion(bf16[16,2048]{1,0:T(8,128)(2,1)S(1)} %get-tuple-element.4, bf16[4096,2048]{1,0:T(8,128)(2,1)} %all-gather.5.cloned.1.call-done), kind=kOutput, calls=%fused_computation.39 | convolution fusion | flops 268435456 | bytes 17104896 | tf_op jit(solution)/shard_map/dot_general | solution.py:39
  325.2 10.2 %convolution_add_fusion = f32[16,4096]{1,0:T(8,128)S(1)} fusion(f32[16,4096]{1,0:T(8,128)S(1)} %fusion.20, bf16[16,2048]{1,0:T(8,128)(2,1)S(1)} %get-tuple-element.6, bf16[4096,2048]{1,0:T(8,128)(2,1)} %all-gather.7.cloned.1.call-done), kind=kOutput, calls=%fused_computation.10 | convolution fusion | flops 268500992 | bytes 17367040 | tf_op jit(solution)/shard_map/dot_general | solution.py:41
  335.4 40.4 %all-reduce.2 = bf16[16,4096]{1,0:T(8,128)(2,1)S(1)} all-reduce(f32[16,4096]{1,0:T(8,128)S(1)} %convolution_add_fusion), channel_id=4, replica_groups=mesh['tp'=8,'dp'=4] {'tp'}, use_global_device_ids=true, to_apply=%region_0.1.clone | all-reduce | flops 65536 | bytes 393216
  376.5 30.5 %multiply_convert_fusion = bf16[4096,2048]{1,0:T(8,128)(2,1)} fusion(bf16[4096,2048]{1,0:T(8,128)(2,1)} %convolution_convert_fusion, bf16[4096,2048]{1,0:T(8,128)(2,1)} %convolution_convert_fusion.1, bf16[4096,2048]{1,0:T(8,128)(2,1)} %convolution_convert_fusion.2, bf16[4096,2048]{1,0:T(8,128)(2,1)} %convolution_convert_fusion.3), kind=kLoop, calls=%fused_computation | loop fusion | flops 75497472 | bytes 83886080 | tf_op jit(solution)/shard_map/convert_element_type | solution.py:65
  407.0 30.5 %multiply_convert_fusion.1 = bf16[4096,2048]{1,0:T(8,128)(2,1)} fusion(bf16[4096,2048]{1,0:T(8,128)(2,1)} %convolution_convert_fusion.4, bf16[4096,2048]{1,0:T(8,128)(2,1)} %convolution_convert_fusion.5, bf16[4096,2048]{1,0:T(8,128)(2,1)} %convolution_convert_fusion.6, bf16[4096,2048]{1,0:T(8,128)(2,1)} %convolution_convert_fusion.7), kind=kLoop, calls=%fused_computation.1 | loop fusion | flops 75497472 | bytes 83886080 | tf_op jit(solution)/shard_map/convert_element_type | solution.py:64
  (12 shorter events, 0.8 us)
Async XLA Ops:
  7.2 221.3 %copy-start = (bf16[1,16,2048]{2,1,0:T(8,128)(2,1)S(1)}, bf16[1,16,2048]{2,1,0:T(8,128)(2,1)}, u32[]{:S(2)}) copy-start(bf16[1,16,2048]{2,1,0:T(8,128)(2,1)} %param.7) | copy-start | bytes 196612
  7.2 113.8 %all-gather.5.cloned.1.call-start = ((), (), s32[]{:S(2)}) async-start(), calls=%async_computation | async-start | bytes 20971520 | tf_op jit(solution)/shard_map/all_gather | solution.py:14
  7.9 220.6 %all-gather.7.cloned.1.call-start = ((), (), s32[]{:S(2)}) async-start(), calls=%async_computation.1 | async-start | bytes 20971520 | tf_op jit(solution)/shard_map/all_gather | solution.py:15
  8.7 8.0 %collective-permute-start = (bf16[1,2,4096]{2,1,0:T(2,128)(2,1)}, bf16[1,2,4096]{2,1,0:T(2,128)(2,1)S(1)}, u32[]{:S(2)}, u32[]{:S(2)}) collective-permute-start(bf16[1,2,4096]{2,1,0:T(2,128)(2,1)} %param.4), channel_id=1, source_target_pairs={{0,4},{4,8},{8,12},{12,16},{16,20},{20,24},{24,28},{28,0},{1,5},{5... | collective-permute-start | bytes 49160 | tf_op jit(solution)/shard_map/ppermute | solution.py:23
  16.7 6.4 %collective-permute-start.1 = (bf16[1,2,4096]{2,1,0:T(2,128)(2,1)S(1)}, bf16[1,2,4096]{2,1,0:T(2,128)(2,1)S(1)}, u32[]{:S(2)}, u32[]{:S(2)}) collective-permute-start(bf16[1,2,4096]{2,1,0:T(2,128)(2,1)S(1)} %collective-permute-done), channel_id=1, source_target_pairs={{0,4},{4,8},{8,12},{12,16},{16,20},{20,24},{24,28},{28,0},{1,5},{5... | collective-permute-start | bytes 49160 | tf_op jit(solution)/shard_map/ppermute | solution.py:23
  23.1 6.4 %collective-permute-start.2 = (bf16[1,2,4096]{2,1,0:T(2,128)(2,1)S(1)}, bf16[1,2,4096]{2,1,0:T(2,128)(2,1)S(1)}, u32[]{:S(2)}, u32[]{:S(2)}) collective-permute-start(bf16[1,2,4096]{2,1,0:T(2,128)(2,1)S(1)} %collective-permute-done.1), channel_id=1, source_target_pairs={{0,4},{4,8},{8,12},{12,16},{16,20},{20,24},{24,28},{28,0},{1,5},{5... | collective-permute-start | bytes 49160 | tf_op jit(solution)/shard_map/ppermute | solution.py:23
  29.5 6.4 %collective-permute-start.3 = (bf16[1,2,4096]{2,1,0:T(2,128)(2,1)S(1)}, bf16[1,2,4096]{2,1,0:T(2,128)(2,1)S(1)}, u32[]{:S(2)}, u32[]{:S(2)}) collective-permute-start(bf16[1,2,4096]{2,1,0:T(2,128)(2,1)S(1)} %collective-permute-done.2), channel_id=1, source_target_pairs={{0,4},{4,8},{8,12},{12,16},{16,20},{20,24},{24,28},{28,0},{1,5},{5... | collective-permute-start | bytes 49160 | tf_op jit(solution)/shard_map/ppermute | solution.py:23
  36.0 6.4 %collective-permute-start.4 = (bf16[1,2,4096]{2,1,0:T(2,128)(2,1)S(1)}, bf16[1,2,4096]{2,1,0:T(2,128)(2,1)S(1)}, u32[]{:S(2)}, u32[]{:S(2)}) collective-permute-start(bf16[1,2,4096]{2,1,0:T(2,128)(2,1)S(1)} %collective-permute-done.3), channel_id=1, source_target_pairs={{0,4},{4,8},{8,12},{12,16},{16,20},{20,24},{24,28},{28,0},{1,5},{5... | collective-permute-start | bytes 49160 | tf_op jit(solution)/shard_map/ppermute | solution.py:23
  42.4 6.4 %collective-permute-start.5 = (bf16[1,2,4096]{2,1,0:T(2,128)(2,1)S(1)}, bf16[1,2,4096]{2,1,0:T(2,128)(2,1)S(1)}, u32[]{:S(2)}, u32[]{:S(2)}) collective-permute-start(bf16[1,2,4096]{2,1,0:T(2,128)(2,1)S(1)} %collective-permute-done.4), channel_id=1, source_target_pairs={{0,4},{4,8},{8,12},{12,16},{16,20},{20,24},{24,28},{28,0},{1,5},{5... | collective-permute-start | bytes 49160 | tf_op jit(solution)/shard_map/ppermute | solution.py:23
  48.9 6.4 %collective-permute-start.6 = (bf16[1,2,4096]{2,1,0:T(2,128)(2,1)S(1)}, bf16[1,2,4096]{2,1,0:T(2,128)(2,1)S(1)}, u32[]{:S(2)}, u32[]{:S(2)}) collective-permute-start(bf16[1,2,4096]{2,1,0:T(2,128)(2,1)S(1)} %collective-permute-done.5), channel_id=1, source_target_pairs={{0,4},{4,8},{8,12},{12,16},{16,20},{20,24},{24,28},{28,0},{1,5},{5... | collective-permute-start | bytes 49160 | tf_op jit(solution)/shard_map/ppermute | solution.py:23
Sparse Core Ops, SparseCore 0:
  9.5 111.4 all-gather.4
  122.6 105.8 all-gather.6
